TPU v7x, 256 devices: a whole 4x4x8 slice. The times are simulated.
256 devices in a mesh: depth: 16 (over x, z_lo), col: 16 (over z_hi, y, core).
Axes of the slice: x: 4, y: 4, z: 8 (z_hi: 2, z_lo: 4; z = z_hi * 4 + z_lo), core: 2. Of those that a mesh axis runs over, the one named last changes fastest.
Arguments:
- recorded: bfloat16 [4, 32, 2, 512, 512], P(None, 'depth', None, 'col'), may hold values from -6 to 6
- vertical: float32 [4, 512], replicated, may hold values from 0.05 to 0.8
Outputs:
- prediction: float32 [4, 2, 512, 512], P(None, None, 'col', 'depth')
All inputs are finite; a program needn't handle non-finite values.
Results may differ from a plain program's by a relative error of at most 0.01.
Values may be sent and summed in bfloat16 or wider, within the bound.
No kernel may reach another device: no remote copies, remote signals or barrier semaphores. Data moves between devices by JAX's collectives and lax.ppermute only.
A program may use at most 64 MiB of HBM per device.

v0:
```python
import jax
import jax.numpy as jnp
from jax import lax
from jax.sharding import PartitionSpec as P


def prefix(x, axis, combine, identity, reverse):
    peers, mine = (lax.axis_size(axis), lax.axis_index(axis))
    everything = lax.all_gather(x, axis)
    start = jnp.broadcast_to(jnp.asarray(identity, x.dtype), x.shape)

    def lap(k, before):
        at = peers - 1 - k if reverse else k
        reached = at > mine if reverse else at < mine
        new = combine(before, everything[at])
        return jnp.where(reached, new, before)

    return lax.fori_loop(0, peers, lap, start)


def from_behind(value, axis, steps):
    count = lax.axis_size(axis)
    initial, last = (max(0, -steps), min(count, count - steps))
    return lax.ppermute(value, axis, [(source, source + steps) for source in range(initial, last)])


def complex_product(left_side, right_side, pattern, stack_axis):
    left_real = left_side[:, :, 0]
    left_imag = left_side[:, :, 1]
    right_real = right_side[:, :, 0]
    right_imag = right_side[:, :, 1]
    real_part = jnp.einsum(
        pattern, left_real, right_real, preferred_element_type=jnp.float32
    ) - jnp.einsum(pattern, left_imag, right_imag, preferred_element_type=jnp.float32)
    imag_part = jnp.einsum(
        pattern, left_real, right_imag, preferred_element_type=jnp.float32
    ) + jnp.einsum(pattern, left_imag, right_real, preferred_element_type=jnp.float32)
    return jnp.stack([real_part, imag_part], axis=stack_axis)


def add_pair(earlier, later):
    return earlier + later


def carry_products(products):
    running = lax.cumsum(products, axis=1)
    before = prefix(running[:, -1], "depth", add_pair, jnp.zeros_like(running[:, -1]), False)
    prefix_all = running + before[:, None]
    previous = from_behind(prefix_all[:, -1], "depth", 1)
    return jnp.concatenate([previous[:, None], prefix_all[:, :-1]], axis=1).astype(jnp.bfloat16)


def shards(recorded, vertical):
    local_depths = recorded.shape[1]
    row_count = recorded.shape[3]
    depth_cells = lax.axis_size("depth") * local_depths
    depth_step = 1.0 / depth_cells
    first_row = lax.axis_index("col") * row_count
    row_wave = lax.dynamic_slice_in_dim(vertical, first_row, row_count, 1)
    depth_f = (
        lax.axis_index("depth") * local_depths + jnp.arange(local_depths, dtype=jnp.int32)
    ).astype(jnp.float32)
    phase_angle = (row_wave[:, None, :, None] + vertical[:, None, None, :]) * depth_f[
        None, :, None, None
    ]
    cosine = jnp.cos(phase_angle)
    sine_part = jnp.sin(phase_angle)
    real_in = recorded[:, :, 0].astype(jnp.float32)
    imag_in = recorded[:, :, 1].astype(jnp.float32)
    plus32 = (
        jnp.stack(
            [real_in * cosine - imag_in * sine_part, real_in * sine_part + imag_in * cosine], axis=2
        )
        * depth_step
    )
    minus_phase = (
        jnp.stack(
            [real_in * cosine + imag_in * sine_part, imag_in * cosine - real_in * sine_part], axis=2
        )
        * depth_step
    ).astype(jnp.bfloat16)
    plus_phase = plus32.astype(jnp.bfloat16)
    inner_sum = lax.cumsum(plus32, axis=1, reverse=True)
    beyond = prefix(inner_sum[:, 0], "depth", add_pair, jnp.zeros_like(inner_sum[:, 0]), True)
    suffix_all = inner_sum + beyond[:, None]
    following = from_behind(suffix_all[:, 0], "depth", -1)
    tail_sum = jnp.concatenate([suffix_all[:, 1:], following[:, None]], axis=1).astype(jnp.bfloat16)
    columns = minus_phase
    products = complex_product(
        columns, lax.all_gather(tail_sum, "col", axis=3, tiled=True), "wzrk,wzkc->wzrc", 2
    )
    lagged = carry_products(products)
    columns = plus_phase
    partial_pred = complex_product(
        columns, lax.all_gather(lagged, "col", axis=3, tiled=True), "wzrk,wzkc->wrc", 1
    )
    return lax.psum_scatter(partial_pred, "depth", scatter_dimension=3, tiled=True)


def solution(mesh):
    in_specs = (P(None, "depth", None, "col", None), P())
    out_specs = P(None, None, "col", "depth")
    return jax.shard_map(shards, mesh=mesh, in_specs=in_specs, out_specs=out_specs, check_vma=False)
```

profile of v0, /device:TPU:8, one launch (start us, length us, event | category | flops | bytes accessed | tf_op | source)
XLA Modules:
  0.0 773.7 jit_solution(15379393343514793894)
XLA Ops:
  9.2 3.1 fusion.51
  13.7 190.7 %all-gather.11.cloned.1.call-done = f32[64,1,2,32,512]{4,3,0,2,1:T(8,128)} async-done(((f32[4,1,2,32,512]{4,3,0,2,1:T(8,128)}), f32[64,1,2,32,512]{4,3,0,2,1:T(8,128)}) %all-gather.11.cloned.1.call-update) | async-done | bytes 8388624 | tf_op jit(solution)/shard_map/all_gather | solution.py:9
  204.4 20.2 %while.30 = (s32[]{:T(128)}, f32[4,2,32,512]{3,2,1,0:T(8,128)S(1)}, s32[]{:T(128)}, f32[16,4,2,32,512]{4,3,1,0,2:T(8,128)}, s32[]{:T(128)}, /*index=5*/s32[]{:T(128)}, s32[]{:T(128)}, s32[]{:T(128)}) while((s32[]{:T(128)}, f32[4,2,32,512]{3,2,1,0:T(8,128)S(1)}, s32[]{:T(128)}, f32[16,4,2,32,512]{4,3,1,0,2:T(8,128)}, s32[]{:T(128)}, ...), condition=%wide.region_2.3_spmd.clone, body=%wide.region_1.2_spmd.clone.sunk | while | flops 393224 | bytes 1573027 | solution.py:18
  205.6 1.2 add_select_fusion.4
  206.9 1.2 add_select_fusion.4
  212.0 1.2 add_select_fusion.4
  213.2 1.2 add_select_fusion.4
  214.5 1.2 add_select_fusion.4
  219.6 1.2 add_select_fusion.4
  220.8 1.2 add_select_fusion.4
  222.1 1.2 add_select_fusion.4
  224.8 1.3 collective-permute-start
  226.1 8.4 %collective-permute-done = bf16[4,2,32,512]{3,2,0,1:T(8,128)(2,1)S(1)} collective-permute-done((bf16[4,2,32,512]{3,2,0,1:T(8,128)(2,1)S(1)}, bf16[4,2,32,512]{3,2,0,1:T(8,128)(2,1)S(1)}, u32[]{:S(2)}, u32[]{:S(2)}) %collective-permute-start) | collective-permute-done | bytes 262176 | tf_op jit(solution)/shard_map/ppermute | solution.py:24
  236.7 106.7 %all-gather.7.cloned.1.call-done = bf16[4,2,2,512,512]{4,3,1,0,2:T(8,128)(2,1)} async-done(((bf16[4,2,2,32,512]{4,3,1,0,2:T(8,128)(2,1)}), bf16[4,2,2,512,512]{4,3,1,0,2:T(8,128)(2,1)}) %all-gather.7.cloned.1.call-update) | async-done | bytes 8388624 | tf_op jit(solution)/shard_map/all_gather | solution.py:90
  343.4 3.1 fusion
  346.5 3.5 fusion.1
  353.0 183.7 %all-gather.13.cloned.1.call-done = f32[64,1,2,32,512]{4,3,1,0,2:T(8,128)} async-done(((f32[4,1,2,32,512]{4,3,1,0,2:T(8,128)}), f32[64,1,2,32,512]{4,3,1,0,2:T(8,128)}) %all-gather.13.cloned.1.call-update) | async-done | bytes 8388624 | tf_op jit(solution)/shard_map/all_gather | solution.py:9
  536.6 20.1 %while.31 = (s32[]{:T(128)}, f32[4,2,32,512]{3,2,1,0:T(8,128)S(1)}, s32[]{:T(128)}, f32[16,4,2,32,512]{4,3,1,0,2:T(8,128)}, s32[]{:T(128)}, /*index=5*/s32[]{:T(128)}) while((s32[]{:T(128)}, f32[4,2,32,512]{3,2,1,0:T(8,128)S(1)}, s32[]{:T(128)}, f32[16,4,2,32,512]{4,3,1,0,2:T(8,128)}, s32[]{:T(128)}, /*index=5*/s32[]{:T(128)}) %tuple.96), condition=%wide.region_5.6_spmd.clone, body=%wide.region_4.5_spmd.clone.sunk | while | flops 393220 | bytes 1572965 | solution.py:18
  557.0 1.3 collective-permute-start.1
  558.3 5.6 collective-permute-done.1
  565.0 109.7 %all-gather.9.cloned.1.call-done = bf16[4,2,2,512,512]{4,3,1,0,2:T(8,128)(2,1)} async-done(((bf16[4,2,2,32,512]{4,3,1,0,2:T(8,128)(2,1)}), bf16[4,2,2,512,512]{4,3,1,0,2:T(8,128)(2,1)}) %all-gather.9.cloned.1.call-update) | async-done | bytes 8388624 | tf_op jit(solution)/shard_map/all_gather | solution.py:95
  674.7 3.8 slice_bitcast_fusion
  682.9 2.0 reshape.30
  685.0 80.6 %reduce-scatter.4.cloned.1.call-done = f32[32,256]{1,0:T(8,128)} async-done(((f32[512,256]{1,0:T(8,128)}), f32[32,256]{1,0:T(8,128)}) %reduce-scatter.4.cloned.1.call-update) | async-done | bytes 32784
  (65 shorter events, 46.1 us)
Async XLA Ops:
  6.5 197.9 %all-gather.11.cloned.1.call-start = ((), (), s32[]{:S(2)}) async-start(), calls=%async_computation.3 | async-start | bytes 8912896 | tf_op jit(solution)/shard_map/all_gather | solution.py:9
  13.6 329.8 %all-gather.7.cloned.1.call-start = ((), (), s32[]{:S(2)}) async-start(), calls=%async_computation.1 | async-start | bytes 8912896 | tf_op jit(solution)/shard_map/all_gather | solution.py:90
  224.8 9.7 %collective-permute-start = (bf16[4,2,32,512]{3,2,0,1:T(8,128)(2,1)S(1)}, bf16[4,2,32,512]{3,2,0,1:T(8,128)(2,1)S(1)}, u32[]{:S(2)}, u32[]{:S(2)}) collective-permute-start(bf16[4,2,32,512]{3,2,0,1:T(8,128)(2,1)S(1)} %get-tuple-element.269), channel_id=1, source_target_pairs={{16,0},{32,16},{48,32},{64,48},{80,64},{96,80},{112,96},{128,112},... | collective-permute-start | bytes 786440 | tf_op jit(solution)/shard_map/ppermute | solution.py:24
  235.4 301.2 %all-gather.13.cloned.1.call-start = ((), (), s32[]{:S(2)}) async-start(), calls=%async_computation.4 | async-start | bytes 8912896 | tf_op jit(solution)/shard_map/all_gather | solution.py:9
  343.4 6.6 copy-start
  352.9 321.8 %all-gather.9.cloned.1.call-start = ((), (), s32[]{:S(2)}) async-start(), calls=%async_computation.2 | async-start | bytes 8912896 | tf_op jit(solution)/shard_map/all_gather | solution.py:95
  557.0 6.9 collective-permute-start.1
  564.8 200.7 %reduce-scatter.4.cloned.1.call-start = ((), (), s32[]{:S(2)}) async-start(), calls=%async_computation.5 | async-start | bytes 557056
Sparse Core Ops, SparseCore 0:
  13.7 190.6 all-gather.10
  235.6 107.7 all-gather.6
  353.0 183.5 all-gather.12
  564.9 109.7 all-gather.8
  685.1 80.4 reduce-scatter.3
where the time goes:
time: 776 us; the launch traced here: 774 us
  waiting for transfers between devices  685 us (88%)
  other arithmetic  47.8 us (6%)
  between operations  13.3 us (2%)
  local copies, waits for them, and re-layouts  12.3 us (2%)
  matrix products  11.2 us (1%)
    all_gather x2, waiting for transfers between devices, prefix(): everything = lax.all_gather(x, axis)  374 us
    all_gather x1, waiting for transfers between devices, shards(): lax.all_gather(lagged, 'col', axis=3, tiled=True)  110 us
    all_gather x1, waiting for transfers between devices, shards(): lax.all_gather(tail_sum, 'col', axis=3, tiled=True)  107 us
    unnamed x6, waiting for transfers between devices  80.7 us
    select_n x32, other arithmetic, lap(): return jnp.where(reached, new, before)  39.5 us
  transfers between devices with their start and end apart: 7, of which 7 were waited for; matrix products, arithmetic and copies ran while one was open for 0% of the time, Pallas kernels for 0%

commit v1 on v0

--- a/solution.py
+++ b/solution.py
@@ -87,7 +87,12 @@
     tail_sum = jnp.concatenate([suffix_all[:, 1:], following[:, None]], axis=1).astype(jnp.bfloat16)
     columns = minus_phase
     products = complex_product(
-        columns, lax.all_gather(tail_sum, "col", axis=3, tiled=True), "wzrk,wzkc->wzrc", 2
+        columns,
+        jnp.concatenate(
+            lax.all_to_all(jnp.stack([tail_sum] * lax.axis_size("col")), "col", 0, 0), axis=3
+        ),
+        "wzrk,wzkc->wzrc",
+        2,
     )
     lagged = carry_products(products)
     columns = plus_phase

time: 776 us -> 922 us (1.19)
  waiting for transfers between devices: 685 us -> 812 us
    all_to_all x0 -> x1, waiting for transfers between devices: none -> 126 us  [shards(): lax.all_to_all(jnp.stack([tail_sum] * lax.axis_size('col')), 'col', 0, 0)]
    all_gather x2, waiting for transfers between devices: 374 us -> 481 us  [prefix(): everything = lax.all_gather(x, axis)]
    all_gather x1 -> x0, waiting for transfers between devices: 107 us -> none  [shards(): lax.all_gather(tail_sum, 'col', axis=3, tiled=True)]
    unnamed x6 -> x5, waiting for transfers between devices: 80.7 us -> 80.8 us
where the time goes in v1:
time: 922 us; the launch traced here: 920 us
  waiting for transfers between devices  812 us (88%)
  other arithmetic  47.1 us (5%)
  local copies, waits for them, and re-layouts  20 us (2%)
  matrix products  16.2 us (2%)
  between operations  13.3 us (1%)
  starting transfers between devices  10.2 us (1%)
    all_gather x2, waiting for transfers between devices, prefix(): everything = lax.all_gather(x, axis)  481 us
    all_to_all x1, waiting for transfers between devices, shards(): lax.all_to_all(jnp.stack([tail_sum] * lax.axis_size('col')), 'col', 0, 0)  126 us
    all_gather x1, waiting for transfers between devices, shards(): lax.all_gather(lagged, 'col', axis=3, tiled=True)  110 us
    unnamed x5, waiting for transfers between devices  80.8 us
    select_n x32, other arithmetic, lap(): return jnp.where(reached, new, before)  39.5 us
  transfers between devices with their start and end apart: 7, of which 7 were waited for; matrix products, arithmetic and copies ran while one was open for 0% of the time, Pallas kernels for 0%

profile of v1, /device:TPU:8, one launch (start us, length us, event | category | flops | bytes accessed | tf_op | source)
XLA Modules:
  0.0 919.5 jit_solution(16265848408180644492)
XLA Ops:
  8.1 4.2 fusion.31
  13.7 190.8 %all-gather.8.cloned.1.call-done = f32[64,1,2,32,512]{4,3,1,0,2:T(8,128)} async-done(((f32[4,1,2,32,512]{4,3,1,0,2:T(8,128)}), f32[64,1,2,32,512]{4,3,1,0,2:T(8,128)}) %all-gather.8.cloned.1.call-update) | async-done | bytes 8388624 | tf_op jit(solution)/shard_map/all_gather | solution.py:9
  204.5 20.2 %while.30 = (s32[]{:T(128)}, f32[4,2,32,512]{3,2,1,0:T(8,128)S(1)}, s32[]{:T(128)}, f32[16,4,2,32,512]{4,3,1,0,2:T(8,128)}, s32[]{:T(128)}, /*index=5*/s32[]{:T(128)}, s32[]{:T(128)}, s32[]{:T(128)}) while((s32[]{:T(128)}, f32[4,2,32,512]{3,2,1,0:T(8,128)S(1)}, s32[]{:T(128)}, f32[16,4,2,32,512]{4,3,1,0,2:T(8,128)}, s32[]{:T(128)}, ...), condition=%wide.region_2.3_spmd.clone, body=%wide.region_1.2_spmd.clone.sunk | while | flops 393224 | bytes 1573027 | solution.py:18
  209.6 1.2 add_select_fusion.4
  210.8 1.2 add_select_fusion.4
  212.1 1.2 add_select_fusion.4
  217.1 1.2 add_select_fusion.4
  224.9 1.3 collective-permute-start
  226.2 8.4 collective-permute-done
  234.8 4.3 stack.20
  239.1 7.5 all-to-all-start
  246.7 125.9 %all-to-all-done = bf16[16,4,2,2,32,512]{5,4,2,1,3,0:T(8,128)(2,1)} async-done(((bf16[16,4,2,2,32,512]{5,4,2,1,3,0:T(8,128)(2,1)}), bf16[16,4,2,2,32,512]{5,4,2,1,3,0:T(8,128)(2,1)}, u32[]{:S(2)}, u32[]{:S(2)}) %all-to-all-start) | async-done | bytes 8388640 | tf_op jit(solution)/shard_map/all_to_all | solution.py:92
  372.7 8.3 copy.19
  380.9 3.1 fusion
  384.1 3.5 fusion.1
  390.5 290.7 %all-gather.10.cloned.1.call-done = f32[64,1,2,32,512]{4,3,1,0,2:T(8,128)} async-done(((f32[4,1,2,32,512]{4,3,1,0,2:T(8,128)}), f32[64,1,2,32,512]{4,3,1,0,2:T(8,128)}) %all-gather.10.cloned.1.call-update) | async-done | bytes 8388624 | tf_op jit(solution)/shard_map/all_gather | solution.py:9
  681.2 20.1 %while.31 = (s32[]{:T(128)}, f32[4,2,32,512]{3,2,1,0:T(8,128)S(1)}, s32[]{:T(128)}, f32[16,4,2,32,512]{4,3,1,0,2:T(8,128)}, s32[]{:T(128)}, /*index=5*/s32[]{:T(128)}) while((s32[]{:T(128)}, f32[4,2,32,512]{3,2,1,0:T(8,128)S(1)}, s32[]{:T(128)}, f32[16,4,2,32,512]{4,3,1,0,2:T(8,128)}, s32[]{:T(128)}, /*index=5*/s32[]{:T(128)}) %tuple.91), condition=%wide.region_5.6_spmd.clone, body=%wide.region_4.5_spmd.clone.sunk | while | flops 393220 | bytes 1572965 | solution.py:18
  701.6 1.3 collective-permute-start.1
  702.9 5.6 collective-permute-done.1
  709.6 109.7 %all-gather.6.cloned.1.call-done = bf16[4,2,2,512,512]{4,3,1,0,2:T(8,128)(2,1)} async-done(((bf16[4,2,2,32,512]{4,3,1,0,2:T(8,128)(2,1)}), bf16[4,2,2,512,512]{4,3,1,0,2:T(8,128)(2,1)}) %all-gather.6.cloned.1.call-update) | async-done | bytes 8388624 | tf_op jit(solution)/shard_map/all_gather | solution.py:100
  819.3 3.1 fusion.13
  822.4 3.5 fusion.12
  828.6 2.0 reshape.47
  830.7 80.7 %reduce-scatter.4.cloned.1.call-done = f32[32,256]{1,0:T(8,128)} async-done(((f32[512,256]{1,0:T(8,128)}), f32[32,256]{1,0:T(8,128)}) %reduce-scatter.4.cloned.1.call-update) | async-done | bytes 32784
  (68 shorter events, 46.4 us)
Async XLA Ops:
  6.5 198.0 %all-gather.8.cloned.1.call-start = ((), (), s32[]{:S(2)}) async-start(), calls=%async_computation.3 | async-start | bytes 8912896 | tf_op jit(solution)/shard_map/all_gather | solution.py:9
  224.9 9.7 %collective-permute-start = (bf16[4,2,32,512]{3,2,0,1:T(8,128)(2,1)S(1)}, bf16[4,2,32,512]{3,2,0,1:T(8,128)(2,1)S(1)}, u32[]{:S(2)}, u32[]{:S(2)}) collective-permute-start(bf16[4,2,32,512]{3,2,0,1:T(8,128)(2,1)S(1)} %get-tuple-element.265), channel_id=1, source_target_pairs={{16,0},{32,16},{48,32},{64,48},{80,64},{96,80},{112,96},{128,112},... | collective-permute-start | bytes 786440 | tf_op jit(solution)/shard_map/ppermute | solution.py:24
  239.1 7.5 copy-start.2
  239.1 133.6 %all-to-all-start = ((bf16[16,4,2,2,32,512]{5,4,2,1,3,0:T(8,128)(2,1)}), bf16[16,4,2,2,32,512]{5,4,2,1,3,0:T(8,128)(2,1)}, u32[]{:S(2)}, u32[]{:S(2)}) async-start(bf16[16,4,2,2,32,512]{5,4,2,1,3,0:T(8,128)(2,1)} %stack.20), calls=%async_computation | async-start | bytes 16777216 | tf_op jit(solution)/shard_map/all_to_all | solution.py:92
  246.6 434.6 %all-gather.10.cloned.1.call-start = ((), (), s32[]{:S(2)}) async-start(), calls=%async_computation.4 | async-start | bytes 8912896 | tf_op jit(solution)/shard_map/all_gather | solution.py:9
  380.9 6.6 copy-start
  390.4 428.8 %all-gather.6.cloned.1.call-start = ((), (), s32[]{:S(2)}) async-start(), calls=%async_computation.2 | async-start | bytes 8912896 | tf_op jit(solution)/shard_map/all_gather | solution.py:100
  701.6 6.9 collective-permute-start.1
  709.4 202.0 %reduce-scatter.4.cloned.1.call-start = ((), (), s32[]{:S(2)}) async-start(), calls=%async_computation.5 | async-start | bytes 557056
  819.3 6.6 copy-start.1
Sparse Core Ops, SparseCore 0:
  13.8 190.6 all-gather.7
  390.6 290.5 all-gather.9
  709.5 109.7 all-gather.5
  830.8 80.5 reduce-scatter.3
